TPU v7x, 256 devices: a whole 4x4x8 slice. The times are simulated.
256 devices in a mesh: dp: 2 (over z_hi), seq: 128 (over y, x, z_lo, core).
Axes of the slice: x: 4, y: 4, z: 8 (z_hi: 2, z_lo: 4; z = z_hi * 4 + z_lo), core: 2. Of those that a mesh axis runs over, the one named last changes fastest.
Arguments:
- signal: bfloat16 [2, 262144, 256], P('dp', 'seq'), may hold values from -6 to 6
- gating: bfloat16 [2, 262144, 256], P('dp', 'seq'), may hold values from -6 to 6
- upstream: bfloat16 [2, 262144, 256], P('dp', 'seq'), may hold values from -1.5 to 1.5
- left_factor: bfloat16 [512, 512, 512], P('seq'), may hold values from -0.25 to 0.25
- right_factor: bfloat16 [512, 512, 512], P('seq'), may hold values from -0.25 to 0.25
Outputs:
- output: bfloat16 [2, 262144, 256], P('dp', 'seq')
- grad_gating: bfloat16 [2, 262144, 256], P('dp', 'seq')
- grad_signal: bfloat16 [2, 262144, 256], P('dp', 'seq')
- grad_left: bfloat16 [512, 512, 512], P('seq')
- grad_right: bfloat16 [512, 512, 512], P('seq')
All inputs are finite; a program needn't handle non-finite values.
Results may differ from a plain program's by a relative error of at most 0.0075.
Values may be sent and summed in bfloat16 or wider, within the bound.
A program may use at most 64 MiB of HBM per device.

v0:
```python
import jax
import jax.numpy as jnp
from jax import lax
from jax.sharding import PartitionSpec as P


def sent_together(arrays, axis, split_dim, concat_dim, along):
    ends, at = ([], 0)
    for a in arrays[:-1]:
        at += a.shape[along]
        ends.append(at)
    both = jnp.concatenate(arrays, axis=along)
    return tuple(
        jnp.split(
            lax.all_to_all(both, axis, split_axis=split_dim, concat_axis=concat_dim, tiled=True),
            ends,
            axis=along,
        )
    )


def over_pieces(x, axis):
    tiles = lax.all_gather(x, axis).astype(jnp.float32)
    return tiles.sum(axis=0)


def column_forward(right_factor, by_column):
    return jnp.einsum(
        "kmi,ikd->mkd", right_factor, by_column, preferred_element_type=jnp.float32
    ).astype(jnp.bfloat16)


def column_backward(right_factor, grad_column):
    return jnp.einsum(
        "kmi,mkd->ikd", right_factor, grad_column, preferred_element_type=jnp.float32
    ).astype(jnp.bfloat16)


def shards(signal, gating, upstream, left_factor, right_factor):
    block_count = left_factor.shape[0]
    block_len = left_factor.shape[1]
    channels = signal.shape[2]
    values = signal.reshape(block_count, block_len, channels)
    gate_rows = gating.reshape(block_count, block_len, channels)
    upstream_rows = upstream.reshape(block_count, block_len, channels)
    mixed_rows = jnp.einsum(
        "ikj,ijd->ikd", left_factor, values, preferred_element_type=jnp.float32
    ).astype(jnp.bfloat16)
    grad_rows = (upstream_rows.astype(jnp.float32) * gate_rows.astype(jnp.float32)).astype(
        jnp.bfloat16
    )
    by_column, grad_column = (
        lax.all_to_all(mixed_rows, "seq", split_axis=1, concat_axis=0, tiled=True),
        lax.all_to_all(grad_rows, "seq", split_axis=1, concat_axis=0, tiled=True),
    )
    second = column_forward(right_factor, by_column)
    grad_second = column_backward(right_factor, grad_column)
    mixed_out, grad_back = sent_together((second, grad_second), "seq", 0, 1, 2)
    mixed_wide = mixed_out.astype(jnp.float32)
    output = (gate_rows.astype(jnp.float32) * mixed_wide).astype(jnp.bfloat16).reshape(signal.shape)
    grad_gate = (
        (upstream_rows.astype(jnp.float32) * mixed_wide).astype(jnp.bfloat16).reshape(signal.shape)
    )
    grad_signal = (
        jnp.einsum("ikj,ikd->ijd", left_factor, grad_back, preferred_element_type=jnp.float32)
        .astype(jnp.bfloat16)
        .reshape(signal.shape)
    )
    left_term = jnp.einsum("ikd,ijd->ikj", grad_back, values, preferred_element_type=jnp.float32)
    right_term = jnp.einsum(
        "mkd,ikd->kmi", grad_column, by_column, preferred_element_type=jnp.float32
    )
    left_sum, right_sum = (
        over_pieces(left_term.astype(jnp.bfloat16), "dp").astype(jnp.float32),
        over_pieces(right_term.astype(jnp.bfloat16), "dp").astype(jnp.float32),
    )
    grad_left = left_sum.astype(jnp.bfloat16)
    grad_right = right_sum.astype(jnp.bfloat16)
    return (output, grad_gate, grad_signal, grad_left, grad_right)


def solution(mesh):
    in_specs = (
        P("dp", "seq", None),
        P("dp", "seq", None),
        P("dp", "seq", None),
        P("seq", None, None),
        P("seq", None, None),
    )
    out_specs = (
        P("dp", "seq", None),
        P("dp", "seq", None),
        P("dp", "seq", None),
        P("seq", None, None),
        P("seq", None, None),
    )
    return jax.shard_map(shards, mesh=mesh, in_specs=in_specs, out_specs=out_specs, check_vma=False)
```

profile of v0, /device:TPU:1, one launch (start us, length us, event | category | flops | bytes accessed | tf_op | source)
XLA Modules:
  0.0 379.8 jit_solution(14072103680214955816)
XLA Ops:
  7.2 0.0 copy-start
  7.2 2.7 convolution_convert_fusion.5
  9.9 0.0 copy-start.2
  9.9 1.8 copy.29
  11.7 14.3 %all-to-all-start = ((bf16[4,512,256]{2,0,1:T(4,128)(2,1)}), bf16[4,512,256]{2,0,1:T(4,128)(2,1)}, u32[]{:S(2)}, u32[]{:S(2)}) async-start(bf16[4,512,256]{2,0,1:T(4,128)(2,1)} %copy.29), calls=%async_computation | async-start | bytes 2097152 | tf_op jit(solution)/shard_map/all_to_all | solution.py:53
  26.0 0.0 copy-done.2
  26.0 1.5 fusion.1
  27.5 1.8 copy.32
  29.2 25.8 %all-to-all-done = bf16[4,512,256]{2,0,1:T(4,128)(2,1)} async-done(((bf16[4,512,256]{2,0,1:T(4,128)(2,1)}), bf16[4,512,256]{2,0,1:T(4,128)(2,1)}, u32[]{:S(2)}, u32[]{:S(2)}) %all-to-all-start) | async-done | bytes 1048608 | tf_op jit(solution)/shard_map/all_to_all | solution.py:53
  55.0 7.5 %all-to-all-start.1 = ((bf16[4,512,256]{2,0,1:T(4,128)(2,1)}), bf16[4,512,256]{2,0,1:T(4,128)(2,1)}, u32[]{:S(2)}, u32[]{:S(2)}) async-start(bf16[4,512,256]{2,0,1:T(4,128)(2,1)} %copy.32), calls=%async_computation.1 | async-start | bytes 2097152 | tf_op jit(solution)/shard_map/all_to_all | solution.py:54
  62.5 1.6 copy.30
  64.2 27.5 %all-to-all-done.1 = bf16[4,512,256]{2,0,1:T(4,128)(2,1)} async-done(((bf16[4,512,256]{2,0,1:T(4,128)(2,1)}), bf16[4,512,256]{2,0,1:T(4,128)(2,1)}, u32[]{:S(2)}, u32[]{:S(2)}) %all-to-all-start.1) | async-done | bytes 1048608 | tf_op jit(solution)/shard_map/all_to_all | solution.py:54
  91.7 1.6 copy.33
  93.3 0.0 copy-start.1
  93.3 0.0 copy-done
  93.3 0.8 fusion.3
  94.1 0.1 copy-done.1
  94.3 0.8 fusion.4
  95.0 1.5 pad_maximum_fusion
  96.5 4.5 %copy.35 = bf16[512,4,512]{2,1,0:T(4,128)(2,1)} copy(bf16[512,4,512]{0,2,1:T(8,128)(2,1)} %pad_maximum_fusion) | data formatting | bytes 4194304 | tf_op jit(solution)/shard_map/concatenate | solution.py:12
  101.0 7.5 %all-to-all-start.2 = ((bf16[512,4,512]{2,1,0:T(4,128)(2,1)}), bf16[512,4,512]{2,1,0:T(4,128)(2,1)}, u32[]{:S(2)}, u32[]{:S(2)}) async-start(bf16[512,4,512]{2,1,0:T(4,128)(2,1)} %copy.35), calls=%async_computation.2 | async-start | bytes 4194304 | tf_op jit(solution)/shard_map/all_to_all | solution.py:15
  108.5 0.2 all-gather.7.cloned.1.call-start
  108.8 3.3 convolution_convert_fusion
  112.1 0.0 all-gather.7.cloned.1.call-update
  112.1 0.0 all-gather.5.cloned.1.call-start
  112.1 137.9 %all-to-all-done.2 = bf16[512,4,512]{2,1,0:T(4,128)(2,1)} async-done(((bf16[512,4,512]{2,1,0:T(4,128)(2,1)}), bf16[512,4,512]{2,1,0:T(4,128)(2,1)}, u32[]{:S(2)}, u32[]{:S(2)}) %all-to-all-start.2) | async-done | bytes 2097184 | tf_op jit(solution)/shard_map/all_to_all | solution.py:15
  250.0 2.8 copy.36
  252.8 2.1 fusion.10
  255.0 1.6 copy.45
  256.6 3.4 convolution_convert_fusion.1
  260.0 0.0 all-gather.5.cloned.1.call-update
  260.0 3.3 fusion.5
  263.3 0.0 copy-start.3
  263.3 2.3 copy.39
  265.6 0.0 copy-done.3
  265.6 3.3 fusion.2
  268.9 0.0 all-gather.7.cloned.1.call-done
  268.9 5.5 %reduce_sum.25 = bf16[4,512,512]{2,1,0:T(8,128)(2,1)} reduce(bf16[2,4,512,512]{3,2,1,0:T(8,128)(2,1)} %bitcast.45, bf16[]{:T(256)} %constant.3.clone.1), dimensions={0}, to_apply=%region_1.0 | reduce | flops 1048576 | bytes 6291458 | tf_op jit(solution)/shard_map/reduce_sum | solution.py:24
  274.4 93.6 %all-gather.5.cloned.1.call-done = bf16[8,512,512]{2,1,0:T(8,128)(2,1)} async-done(((bf16[4,512,512]{2,1,0:T(8,128)(2,1)}), bf16[8,512,512]{2,1,0:T(8,128)(2,1)}) %all-gather.5.cloned.1.call-update) | async-done | bytes 4194320 | tf_op jit(solution)/shard_map/all_gather | solution.py:23
  368.0 4.9 %reduce_sum.24 = bf16[4,512,512]{2,1,0:T(8,128)(2,1)} reduce(bf16[2,4,512,512]{3,2,1,0:T(8,128)(2,1)} %bitcast.46, bf16[]{:T(256)} %constant.3.clone.1), dimensions={0}, to_apply=%region_0.0 | reduce | flops 1048576 | bytes 6291458 | tf_op jit(solution)/shard_map/reduce_sum | solution.py:24
Async XLA Ops:
  7.2 86.2 %copy-start = (bf16[4,512,512]{2,1,0:T(8,128)(2,1)S(1)}, bf16[4,512,512]{2,1,0:T(8,128)(2,1)}, u32[]{:S(2)}) copy-start(bf16[4,512,512]{2,1,0:T(8,128)(2,1)} %param.9) | copy-start | bytes 6291460
  9.9 16.1 %copy-start.2 = (bf16[1,2048,256]{2,1,0:T(8,128)(2,1)S(1)}, bf16[1,2048,256]{2,1,0:T(8,128)(2,1)}, u32[]{:S(2)}) copy-start(bf16[1,2048,256]{2,1,0:T(8,128)(2,1)} %param.7) | copy-start | bytes 3145732
  11.7 43.3 %all-to-all-start = ((bf16[4,512,256]{2,0,1:T(4,128)(2,1)}), bf16[4,512,256]{2,0,1:T(4,128)(2,1)}, u32[]{:S(2)}, u32[]{:S(2)}) async-start(bf16[4,512,256]{2,0,1:T(4,128)(2,1)} %copy.29), calls=%async_computation | async-start | bytes 2097152 | tf_op jit(solution)/shard_map/all_to_all | solution.py:53
  55.0 36.7 %all-to-all-start.1 = ((bf16[4,512,256]{2,0,1:T(4,128)(2,1)}), bf16[4,512,256]{2,0,1:T(4,128)(2,1)}, u32[]{:S(2)}, u32[]{:S(2)}) async-start(bf16[4,512,256]{2,0,1:T(4,128)(2,1)} %copy.32), calls=%async_computation.1 | async-start | bytes 2097152 | tf_op jit(solution)/shard_map/all_to_all | solution.py:54
  93.3 1.0 copy-start.1
  101.0 149.0 %all-to-all-start.2 = ((bf16[512,4,512]{2,1,0:T(4,128)(2,1)}), bf16[512,4,512]{2,1,0:T(4,128)(2,1)}, u32[]{:S(2)}, u32[]{:S(2)}) async-start(bf16[512,4,512]{2,1,0:T(4,128)(2,1)} %copy.35), calls=%async_computation.2 | async-start | bytes 4194304 | tf_op jit(solution)/shard_map/all_to_all | solution.py:15
  108.5 160.4 %all-gather.7.cloned.1.call-start = ((), (), s32[]{:S(2)}) async-start(), calls=%async_computation.4 | async-start | bytes 6291456 | tf_op jit(solution)/shard_map/all_gather | solution.py:23
  112.1 255.9 %all-gather.5.cloned.1.call-start = ((), (), s32[]{:S(2)}) async-start(), calls=%async_computation.3 | async-start | bytes 6291456 | tf_op jit(solution)/shard_map/all_gather | solution.py:23
  263.3 2.4 copy-start.3
Sparse Core Ops, SparseCore 0:
  112.2 124.3 all-gather.6
  260.1 107.8 all-gather.4
where the time goes:
time: 381 us; the launch traced here: 380 us
  waiting for transfers between devices  285 us (75%)
  starting transfers between devices  29.6 us (8%)
  local copies, waits for them, and re-layouts  20.4 us (5%)
  other arithmetic  16.7 us (4%)
  matrix products  14.2 us (4%)
  between operations  14.2 us (4%)
    all_to_all x1, waiting for transfers between devices, sent_together(): lax.all_to_all(both, axis, split_axis=split_dim, concat_axis=concat_dim,...  138 us
    all_gather x2, waiting for transfers between devices, over_pieces(): tiles = lax.all_gather(x, axis).astype(jnp.float32)  93.6 us
    all_to_all x1, waiting for transfers between devices, shards(): lax.all_to_all(grad_rows, 'seq', split_axis=1, concat_axis=0, tiled=True)  27.5 us
    all_to_all x1, waiting for transfers between devices, shards(): lax.all_to_all(mixed_rows, 'seq', split_axis=1, concat_axis=0, tiled=True)  25.8 us
    all_to_all x1, starting transfers between devices, shards(): lax.all_to_all(mixed_rows, 'seq', split_axis=1, concat_axis=0, tiled=True)  14.3 us
    reduce_sum x2, other arithmetic, over_pieces(): return tiles.sum(axis=0)  10.4 us
  transfers between devices with their start and end apart: 5, of which 4 were waited for; matrix products, arithmetic and copies ran while one was open for 9% of the time, Pallas kernels for 0%

commit v1 on v0

--- a/solution.py
+++ b/solution.py
@@ -2,6 +2,7 @@
 import jax.numpy as jnp
 from jax import lax
 from jax.sharding import PartitionSpec as P
+from jax.lax import all_to_all, axis_size
 
 
 def sent_together(arrays, axis, split_dim, concat_dim, along):
@@ -51,7 +52,9 @@
     )
     by_column, grad_column = (
         lax.all_to_all(mixed_rows, "seq", split_axis=1, concat_axis=0, tiled=True),
-        lax.all_to_all(grad_rows, "seq", split_axis=1, concat_axis=0, tiled=True),
+        jnp.concatenate(
+            all_to_all(jnp.stack(jnp.split(grad_rows, axis_size("seq"), axis=1)), "seq", 0, 0), 0
+        ),
     )
     second = column_forward(right_factor, by_column)
     grad_second = column_backward(right_factor, grad_column)

time: 381 us -> 379 us (level)
  no operation moved by 1% of the time
where the time goes in v1:
time: 379 us; the launch traced here: 378 us
  waiting for transfers between devices  283 us (75%)
  starting transfers between devices  28.7 us (8%)
  local copies, waits for them, and re-layouts  21 us (6%)
  other arithmetic  16.7 us (4%)
  between operations  14.7 us (4%)
  matrix products  14.2 us (4%)
    all_to_all x1, waiting for transfers between devices, sent_together(): lax.all_to_all(both, axis, split_axis=split_dim, concat_axis=concat_dim,...  138 us
    all_gather x2, waiting for transfers between devices, over_pieces(): tiles = lax.all_gather(x, axis).astype(jnp.float32)  93.6 us
    all_to_all x1, waiting for transfers between devices, shards(): all_to_all(jnp.stack(jnp.split(grad_rows, axis_size('seq'), axis=1)), 'se...  26.8 us
    all_to_all x1, waiting for transfers between devices, shards(): lax.all_to_all(mixed_rows, 'seq', split_axis=1, concat_axis=0, tiled=True)  24.3 us
    all_to_all x1, starting transfers between devices, shards(): lax.all_to_all(mixed_rows, 'seq', split_axis=1, concat_axis=0, tiled=True)  14.3 us
    reduce_sum x2, other arithmetic, over_pieces(): return tiles.sum(axis=0)  10.4 us
  transfers between devices with their start and end apart: 5, of which 4 were waited for; matrix products, arithmetic and copies ran while one was open for 9% of the time, Pallas kernels for 0%

profile of v1, /device:TPU:1, one launch (start us, length us, event | category | flops | bytes accessed | tf_op | source)
XLA Modules:
  0.0 377.9 jit_solution(4375716928952038583)
XLA Ops:
  7.2 0.0 copy-start
  7.2 2.7 convolution_convert_fusion.5
  9.9 0.0 copy-start.2
  9.9 1.8 copy.27
  11.7 14.3 %all-to-all-start = ((bf16[4,512,256]{2,0,1:T(4,128)(2,1)}), bf16[4,512,256]{2,0,1:T(4,128)(2,1)}, u32[]{:S(2)}, u32[]{:S(2)}) async-start(bf16[4,512,256]{2,0,1:T(4,128)(2,1)} %copy.27), calls=%async_computation | async-start | bytes 2097152 | tf_op jit(solution)/shard_map/all_to_all | solution.py:54
  26.0 0.0 copy-done.2
  26.0 1.5 fusion.1
  29.8 0.0 copy-start.4
  29.8 1.0 copy-done.4
  30.8 24.3 %all-to-all-done = bf16[4,512,256]{2,0,1:T(4,128)(2,1)} async-done(((bf16[4,512,256]{2,0,1:T(4,128)(2,1)}), bf16[4,512,256]{2,0,1:T(4,128)(2,1)}, u32[]{:S(2)}, u32[]{:S(2)}) %all-to-all-start) | async-done | bytes 1048608 | tf_op jit(solution)/shard_map/all_to_all | solution.py:54
  55.0 6.7 %all-to-all-start.1 = ((bf16[128,4,4,256]{3,2,1,0:T(4,128)(2,1)}), bf16[128,4,4,256]{3,2,1,0:T(4,128)(2,1)S(1)}, u32[]{:S(2)}, u32[]{:S(2)}) async-start(bf16[128,4,4,256]{3,2,1,0:T(4,128)(2,1)} %copy-done.4), calls=%async_computation.1 | async-start | bytes 2097152 | tf_op jit(solution)/shard_map/all_to_all | solution.py:56
  61.7 2.6 copy.28
  64.3 26.8 %all-to-all-done.1 = bf16[128,4,4,256]{3,2,1,0:T(4,128)(2,1)S(1)} async-done(((bf16[128,4,4,256]{3,2,1,0:T(4,128)(2,1)}), bf16[128,4,4,256]{3,2,1,0:T(4,128)(2,1)S(1)}, u32[]{:S(2)}, u32[]{:S(2)}) %all-to-all-start.1) | async-done | bytes 1048608 | tf_op jit(solution)/shard_map/all_to_all | solution.py:56
  91.1 0.0 copy-done
  91.1 0.0 copy-start.1
  91.1 0.8 fusion.4
  91.8 0.5 copy-done.1
  92.3 0.8 fusion.3
  93.1 1.5 pad_maximum_fusion
  94.6 4.5 %copy.31 = bf16[512,4,512]{2,1,0:T(4,128)(2,1)} copy(bf16[512,4,512]{0,2,1:T(8,128)(2,1)} %pad_maximum_fusion) | data formatting | bytes 4194304 | tf_op jit(solution)/shard_map/concatenate | solution.py:13
  99.1 7.5 %all-to-all-start.2 = ((bf16[512,4,512]{2,1,0:T(4,128)(2,1)}), bf16[512,4,512]{2,1,0:T(4,128)(2,1)}, u32[]{:S(2)}, u32[]{:S(2)}) async-start(bf16[512,4,512]{2,1,0:T(4,128)(2,1)} %copy.31), calls=%async_computation.2 | async-start | bytes 4194304 | tf_op jit(solution)/shard_map/all_to_all | solution.py:16
  106.6 0.2 all-gather.7.cloned.1.call-start
  106.8 3.3 convolution_convert_fusion
  110.1 0.0 all-gather.7.cloned.1.call-update
  110.2 0.0 all-gather.5.cloned.1.call-start
  110.2 137.9 %all-to-all-done.2 = bf16[512,4,512]{2,1,0:T(4,128)(2,1)} async-done(((bf16[512,4,512]{2,1,0:T(4,128)(2,1)}), bf16[512,4,512]{2,1,0:T(4,128)(2,1)}, u32[]{:S(2)}, u32[]{:S(2)}) %all-to-all-start.2) | async-done | bytes 2097184 | tf_op jit(solution)/shard_map/all_to_all | solution.py:16
  248.1 2.8 copy.32
  250.9 2.1 fusion.10
  253.1 1.6 copy.41
  254.7 3.4 convolution_convert_fusion.1
  258.0 0.0 all-gather.5.cloned.1.call-update
  258.1 3.3 fusion.5
  261.3 0.0 copy-start.3
  261.3 2.3 copy.35
  263.7 0.0 copy-done.3
  263.7 3.3 fusion.2
  267.0 0.0 all-gather.7.cloned.1.call-done
  267.0 5.5 %reduce_sum.25 = bf16[4,512,512]{2,1,0:T(8,128)(2,1)} reduce(bf16[2,4,512,512]{3,2,1,0:T(8,128)(2,1)} %bitcast.554, bf16[]{:T(256)} %constant.3.clone.1), dimensions={0}, to_apply=%region_1.0 | reduce | flops 1048576 | bytes 6291458 | tf_op jit(solution)/shard_map/reduce_sum | solution.py:25
  272.5 93.6 %all-gather.5.cloned.1.call-done = bf16[8,512,512]{2,1,0:T(8,128)(2,1)} async-done(((bf16[4,512,512]{2,1,0:T(8,128)(2,1)}), bf16[8,512,512]{2,1,0:T(8,128)(2,1)}) %all-gather.5.cloned.1.call-update) | async-done | bytes 4194320 | tf_op jit(solution)/shard_map/all_gather | solution.py:24
  366.1 4.9 %reduce_sum.24 = bf16[4,512,512]{2,1,0:T(8,128)(2,1)} reduce(bf16[2,4,512,512]{3,2,1,0:T(8,128)(2,1)} %bitcast.555, bf16[]{:T(256)} %constant.3.clone.1), dimensions={0}, to_apply=%region_0.0 | reduce | flops 1048576 | bytes 6291458 | tf_op jit(solution)/shard_map/reduce_sum | solution.py:25
  (128 shorter events, 1.8 us)
Async XLA Ops:
  7.2 83.9 %copy-start = (bf16[4,512,512]{2,1,0:T(8,128)(2,1)S(1)}, bf16[4,512,512]{2,1,0:T(8,128)(2,1)}, u32[]{:S(2)}) copy-start(bf16[4,512,512]{2,1,0:T(8,128)(2,1)} %param.9) | copy-start | bytes 6291460
  9.9 16.1 %copy-start.2 = (bf16[1,2048,256]{2,1,0:T(8,128)(2,1)S(1)}, bf16[1,2048,256]{2,1,0:T(8,128)(2,1)}, u32[]{:S(2)}) copy-start(bf16[1,2048,256]{2,1,0:T(8,128)(2,1)} %param.7) | copy-start | bytes 3145732
  11.7 43.3 %all-to-all-start = ((bf16[4,512,256]{2,0,1:T(4,128)(2,1)}), bf16[4,512,256]{2,0,1:T(4,128)(2,1)}, u32[]{:S(2)}, u32[]{:S(2)}) async-start(bf16[4,512,256]{2,0,1:T(4,128)(2,1)} %copy.27), calls=%async_computation | async-start | bytes 2097152 | tf_op jit(solution)/shard_map/all_to_all | solution.py:54
  29.8 1.0 copy-start.4
  55.0 36.1 %all-to-all-start.1 = ((bf16[128,4,4,256]{3,2,1,0:T(4,128)(2,1)}), bf16[128,4,4,256]{3,2,1,0:T(4,128)(2,1)S(1)}, u32[]{:S(2)}, u32[]{:S(2)}) async-start(bf16[128,4,4,256]{3,2,1,0:T(4,128)(2,1)} %copy-done.4), calls=%async_computation.1 | async-start | bytes 2097152 | tf_op jit(solution)/shard_map/all_to_all | solution.py:56
  91.1 1.2 copy-start.1
  99.1 149.0 %all-to-all-start.2 = ((bf16[512,4,512]{2,1,0:T(4,128)(2,1)}), bf16[512,4,512]{2,1,0:T(4,128)(2,1)}, u32[]{:S(2)}, u32[]{:S(2)}) async-start(bf16[512,4,512]{2,1,0:T(4,128)(2,1)} %copy.31), calls=%async_computation.2 | async-start | bytes 4194304 | tf_op jit(solution)/shard_map/all_to_all | solution.py:16
  106.6 160.4 %all-gather.7.cloned.1.call-start = ((), (), s32[]{:S(2)}) async-start(), calls=%async_computation.4 | async-start | bytes 6291456 | tf_op jit(solution)/shard_map/all_gather | solution.py:24
  110.2 255.9 %all-gather.5.cloned.1.call-start = ((), (), s32[]{:S(2)}) async-start(), calls=%async_computation.3 | async-start | bytes 6291456 | tf_op jit(solution)/shard_map/all_gather | solution.py:24
  261.3 2.4 copy-start.3
Sparse Core Ops, SparseCore 0:
  110.3 124.3 all-gather.6
  258.2 107.8 all-gather.4
